TPU v7x, 128 devices: a whole 4x4x4 slice. The times are simulated.
128 devices in a mesh: row: 16 (over x, y_hi, core), col: 8 (over z, y_lo).
Axes of the slice: x: 4, y: 4 (y_hi: 2, y_lo: 2; y = y_hi * 2 + y_lo), z: 4, core: 2. Of those that a mesh axis runs over, the one named last changes fastest.
Arguments:
- database: bfloat16 [8192, 32768], P('row', 'col'), may hold values from -1 to 1
- query: bfloat16 [256, 8192], P('col', 'row'), may hold values from -8 to 8
- slot_map: int32 [256], replicated, may hold values from 0 to 255, each once
- keys: bfloat16 [256, 2048, 512], P(('row', 'col')), may hold values from -0.125 to 0.125
Outputs:
- packed: float32 [256, 16, 512], P(('row', 'col'))
Inputs may be any that keep to these rules, and one draw needn't show every extreme that they name: `slot_map`: each slot serves a different client.
All inputs are finite; a program needn't handle non-finite values.
Results may differ from a plain program's by a relative error of at most 0.0085.
Values may be sent and summed in bfloat16 or wider, within the bound.
A program may use at most 64 MiB of HBM per device.

v0:
```python
import jax
import jax.numpy as jnp
from jax import lax
from jax.sharding import Mesh
from jax.sharding import PartitionSpec as P

ROW = ("row_0", "row_1", "row_2")
ROW_COL = ("row_0", "row_1", "row_2", "col")


def joined_along(blocks, dim):
    blocks = jnp.moveaxis(blocks, 0, dim)
    lengths = blocks.shape
    return blocks.reshape(*lengths[:dim], lengths[dim] * lengths[dim + 1], *lengths[dim + 2 :])


def from_everyone(x, axis):
    devices = lax.axis_size(axis)
    return lax.all_to_all(jnp.broadcast_to(x[None], (devices, *x.shape)), axis, 0, 0, tiled=True)


def gathered_copies(x, axis, dim):
    return joined_along(from_everyone(x, axis), dim)


def cut_along(x, dim, devices):
    before, after = (x.shape[:dim], x.shape[dim + 1 :])
    return jnp.moveaxis(x.reshape(*before, devices, -1, *after), dim, 0)


def summed_on_arrival(x, axis, dim):
    devices = lax.axis_size(axis)
    blocks = lax.all_to_all(cut_along(x, dim, devices), axis, 0, 0, tiled=True)
    return jnp.sum(blocks, axis=0)


def sum_by_axis(x, axes, dim):
    far, near = axes
    blocks = cut_along(x, dim, lax.axis_size(far))
    nearer = summed_on_arrival(blocks, near, dim + 1)
    arrived = lax.all_to_all(nearer, far, split_axis=0, concat_axis=0, tiled=True)
    return arrived.sum(axis=0)


def shards(database, query, slot_map, keys):
    rows_axis = lax.axis_size(ROW)
    cols_axis = lax.axis_size("col")
    factor = float(database.shape[0] * rows_axis) ** (-0.5)
    gathered = gathered_copies(query, "col", 0)
    total = gathered.shape[0]
    owned_count = total // (rows_axis * cols_axis)
    chosen = jnp.take(gathered, slot_map, axis=0)
    partial_value = jnp.dot(chosen, database, preferred_element_type=jnp.float32)
    block = sum_by_axis(partial_value, (("row_0", "row_1"), "row_2"), 0)
    owned = lax.all_to_all(
        block.astype(jnp.bfloat16), "col", split_axis=0, concat_axis=1, tiled=True
    ).astype(block.dtype)
    switched = (owned * factor).astype(jnp.bfloat16)
    tiles = switched.reshape(owned_count, -1, keys.shape[1])
    return jnp.einsum("ptj,pjk->ptk", tiles, keys, preferred_element_type=jnp.float32)


def solution(mesh):
    torus = Mesh(
        mesh.devices.reshape(4, 2, 2, mesh.shape["col"]), ("row_0", "row_1", "row_2", "col")
    )
    return jax.shard_map(
        shards,
        mesh=torus,
        in_specs=(P(ROW, "col"), P("col", ROW), P(), P(ROW_COL, None, None)),
        out_specs=P(ROW_COL, None, None),
        check_vma=False,
    )
```

profile of v0, /device:TPU:0, one launch (start us, length us, event | category | flops | bytes accessed | tf_op | source)
XLA Modules:
  0.0 80.7 jit_solution(5123270558482886548)
XLA Ops:
  0.0 1.5 %broadcast_in_dim.19 = bf16[8,32,512]{2,1,0:T(8,128)(2,1)} broadcast(bf16[32,512]{1,0:T(8,128)(2,1)} %param.5), dimensions={1,2} | broadcast | bytes 294912 | tf_op jit(solution)/shard_map/broadcast_in_dim | solution.py:19
  1.5 6.4 %all-to-all-start = ((bf16[8,32,512]{2,1,0:T(8,128)(2,1)}), bf16[8,32,512]{2,1,0:T(8,128)(2,1)S(1)}, u32[]{:S(2)}, u32[]{:S(2)}) async-start(bf16[8,32,512]{2,1,0:T(8,128)(2,1)} %broadcast_in_dim.19), calls=%async_computation | async-start | bytes 524288 | tf_op jit(solution)/shard_map/all_to_all | solution.py:19
  7.9 0.7 compare_select_fusion
  8.6 0.7 compare_and_fusion
  9.3 5.9 %all-to-all-done = bf16[8,32,512]{2,1,0:T(8,128)(2,1)S(1)} async-done(((bf16[8,32,512]{2,1,0:T(8,128)(2,1)}), bf16[8,32,512]{2,1,0:T(8,128)(2,1)S(1)}, u32[]{:S(2)}, u32[]{:S(2)}) %all-to-all-start) | async-done | bytes 262176 | tf_op jit(solution)/shard_map/all_to_all | solution.py:19
  15.2 1.2 %gather_fusion = bf16[256,512]{1,0:T(8,128)(2,1)S(1)} fusion(bf16[256,512]{1,0:T(8,128)(2,1)S(1)} %bitcast.10, s32[1024]{0:T(1024)S(1)} %pad_clamp_fusion), kind=kCustom, calls=%fused_computation | custom fusion | bytes 525312 | tf_op jit(solution)/shard_map/jit(_take)/gather | solution.py:52
  16.3 3.5 %fusion = f32[256,4096]{1,0:T(8,128)S(1)} fusion(bf16[512,4096]{1,0:T(8,128)(2,1)} %param.4, bf16[256,512]{1,0:T(8,128)(2,1)S(1)} %gather_fusion, pred[256]{0:T(512)(128)(4,1)S(1)} %compare_and_fusion), kind=kOutput, calls=%fused_computation.3 | convolution fusion | flops 1073872896 | bytes 8651008 | tf_op jit(solution)/shard_map/dot_general | solution.py:53
  19.8 0.4 copy.11
  20.3 8.2 %all_to_all.25 = f32[2,8,16,4096]{3,2,1,0:T(8,128)} all-to-all(f32[2,8,16,4096]{3,2,1,0:T(8,128)S(1)} %bitcast.12), channel_id=1, replica_groups=mesh['row_0'=4,'row_1'=2,'row_2'=2,'col'=8] {'row_2'}, dimensions={0} | all-to-all | bytes 8388608 | tf_op jit(solution)/shard_map/all_to_all | solution.py:33
  28.4 2.7 %reduce_sum.18 = f32[8,16,4096]{2,1,0:T(8,128)S(1)} reduce(f32[2,8,16,4096]{3,2,1,0:T(8,128)} %all_to_all.25, f32[]{:T(128)} %constant.18.clone.1), dimensions={0}, to_apply=%region_0.1 | reduce | flops 524288 | bytes 6291460 | tf_op jit(solution)/shard_map/reduce_sum | solution.py:34
  31.1 34.9 %all_to_all.26 = f32[8,16,4096]{2,1,0:T(8,128)} all-to-all(f32[8,16,4096]{2,1,0:T(8,128)S(1)} %reduce_sum.18), channel_id=1, replica_groups=mesh['row_0'=4,'row_1'=2,'row_2'=2,'col'=8] {'row_0','row_1'}, dimensions={0} | all-to-all | bytes 4194304 | tf_op jit(solution)/shard_map/all_to_all | solution.py:41
  66.0 1.7 %reduce_sum.19 = bf16[16,4096]{1,0:T(8,128)(2,1)S(1)} reduce(f32[8,16,4096]{2,1,0:T(8,128)} %all_to_all.26, f32[]{:T(128)} %constant.18.clone.1), dimensions={0}, to_apply=%region_1.2 | reduce | flops 458752 | bytes 2228228 | tf_op jit(solution)/shard_map/reduce_sum | solution.py:42
  67.8 0.1 convert_element_type.24
  67.9 9.1 %all_to_all.27 = bf16[8,2,4096]{2,1,0:T(2,128)(2,1)S(1)} all-to-all(bf16[8,2,4096]{2,1,0:T(2,128)(2,1)S(1)} %convert_element_type.24), channel_id=1, replica_groups=mesh['row_0'=4,'row_1'=2,'row_2'=2,'col'=8] {'col'}, dimensions={0} | all-to-all | bytes 262144 | tf_op jit(solution)/shard_map/all_to_all | solution.py:55
  76.9 0.1 fusion.3
  77.1 0.1 copy.9
  77.2 0.1 convert_element_type.28
  77.2 3.5 %fusion.6 = f32[2,16,512]{2,1,0:T(8,128)} fusion(bf16[2,16,2048]{2,1,0:T(8,128)(2,1)S(1)} %convert_element_type.28, bf16[2,2048,512]{2,1,0:T(8,128)(2,1)} %param.7), kind=kOutput, calls=%fused_computation.12 | convolution fusion | flops 67108864 | bytes 4390912 | tf_op jit(solution)/shard_map/ptj,pjk->ptk/dot_general | solution.py:60
  (1 shorter events, 0.0 us)
Async XLA Ops:
  1.5 13.7 %all-to-all-start = ((bf16[8,32,512]{2,1,0:T(8,128)(2,1)}), bf16[8,32,512]{2,1,0:T(8,128)(2,1)S(1)}, u32[]{:S(2)}, u32[]{:S(2)}) async-start(bf16[8,32,512]{2,1,0:T(8,128)(2,1)} %broadcast_in_dim.19), calls=%async_computation | async-start | bytes 524288 | tf_op jit(solution)/shard_map/all_to_all | solution.py:19
where the time goes:
time: 81.3 us; the launch traced here: 80.7 us
  blocking collectives  52.2 us (64%)
  matrix products  6.96 us (9%)
  starting transfers between devices  6.41 us (8%)
  waiting for transfers between devices  5.91 us (7%)
  other arithmetic  5.89 us (7%)
  local copies, waits for them, and re-layouts  3.3 us (4%)
    all_to_all x1, blocking collectives, sum_by_axis(): lax.all_to_all(nearer, far, split_axis=0, concat_axis=0, tiled=True)  34.9 us
    all_to_all x1, blocking collectives, shards(): lax.all_to_all(block.astype(jnp.bfloat16), 'col', split_axis=0, concat_ax...  9.08 us
    all_to_all x1, blocking collectives, summed_on_arrival(): blocks = lax.all_to_all(cut_along(x, dim, devices), axis, 0, 0, tiled=True)  8.17 us
    all_to_all x1, starting transfers between devices, from_everyone(): lax.all_to_all(jnp.broadcast_to(x[None], (devices, *x.shape)), axis, 0, 0...  6.41 us
    all_to_all x1, waiting for transfers between devices, from_everyone(): lax.all_to_all(jnp.broadcast_to(x[None], (devices, *x.shape)), axis, 0, 0...  5.91 us
    dot_general x1, matrix products, shards(): jnp.dot(chosen, database, preferred_element_type=jnp.float32)  3.48 us
    dot_general x1, matrix products, shards(): jnp.einsum('ptj,pjk->ptk', tiles, keys, preferred_element_type=jnp.float32)  3.48 us
    reduce_sum x1, other arithmetic, summed_on_arrival(): return jnp.sum(blocks, axis=0)  2.68 us
  transfers between devices with their start and end apart: 1, of which 1 were waited for; matrix products, arithmetic and copies ran while one was open for 2% of the time, Pallas kernels for 0%

commit v1 on v0

v1 whole, which is shorter than its diff:
```python
import functools

import jax
import jax.numpy as jnp
from jax import lax
from jax.experimental import pallas as pl
from jax.experimental.pallas import tpu as pltpu
from jax.sharding import PartitionSpec as P

MESH = pl.DeviceIdType.MESH
CHUNKS = 4
F32 = jnp.float32
BF16 = jnp.bfloat16


def place():
    row, col = lax.axis_index("row"), lax.axis_index("col")
    x, y_hi, core = row // 4, lax.rem(row // 2, 2), lax.rem(row, 2)
    z, y_lo = col // 2, lax.rem(col, 2)
    return x, 2 * y_hi + y_lo, z, core


def device(x, y, z, core):
    x, y, z = lax.rem(x, 4), lax.rem(y, 4), lax.rem(z, 4)
    return ((2 * x + y // 2) * 2 + core, 2 * z + lax.rem(y, 2))


def kernel(
    factor,
    slot_hbm,
    query_hbm,
    db_hbm,
    keys_hbm,
    out_ref,
    slots,
    gathered,
    db,
    keys,
    core_out,
    core_in,
    own,
    far_out,
    far_in,
    near_out,
    near_in,
    spread,
    send_out,
    arrived,
    switched,
    local_sem,
    db_sem,
    keys_sem,
    query_sems,
    core_sems,
    far_sems,
    near_sems,
    owner_sems,
):
    x, y, z, core = place()
    y_hi, y_lo = y // 2, lax.rem(y, 2)
    col = 2 * z + y_lo
    depth = keys_hbm.shape[1] // CHUNKS
    lane_groups = depth // 128

    def remote(src, dst, sems, index, target):
        return pltpu.make_async_remote_copy(
            src_ref=src,
            dst_ref=dst,
            send_sem=sems.at[(0, *index)],
            recv_sem=sems.at[(1, *index)],
            device_id=target,
            device_id_type=MESH,
        )

    slot_copy = pltpu.make_async_copy(slot_hbm, slots, local_sem.at[0])
    slot_copy.start()
    own_query = pltpu.make_async_copy(query_hbm, gathered.at[col], local_sem.at[1])
    own_query.start()
    db_copies = []
    for k in range(CHUNKS):
        for t in range(2):
            start = t * keys_hbm.shape[1] + k * depth
            copy = pltpu.make_async_copy(
                db_hbm.at[:, pl.ds(start, depth)],
                db.at[k, :, pl.ds(t * depth, depth)],
                db_sem.at[k, t],
            )
            copy.start()
            db_copies.append(copy)
    key_copies = []
    for k in range(CHUNKS):
        copy = pltpu.make_async_copy(
            keys_hbm.at[:, pl.ds(k * depth, depth), :], keys.at[k], keys_sem.at[k]
        )
        copy.start()
        key_copies.append(copy)

    partner = device(x, y, z, 1 - core)
    right, left = device(x + 1, y, z, core), device(x + 3, y, z, core)
    owners = [device(x, y + b // 4, z + b % 4, core) for b in range(16)]
    column_peers = []
    for other in range(2):
        peer_y = 2 * y_hi + (y_lo if other == 0 else 1 - y_lo)
        for dz in (2, 1, 3, 0):
            if other or dz:
                column_peers.append(device(x, peer_y, z + dz, core))

    barrier = pltpu.get_barrier_semaphore()
    greeted = [partner, right, left, *owners[1:]]
    for target in greeted:
        pl.semaphore_signal(barrier, inc=1, device_id=target, device_id_type=MESH)
    pl.semaphore_wait(barrier, len(greeted))

    query_copies = []
    for i, target in enumerate(column_peers):
        copy = remote(query_hbm, gathered.at[col], query_sems, (i,), target)
        copy.start()
        query_copies.append(copy)

    slot_copy.wait()
    total = slots.shape[1]
    line = lax.broadcasted_iota(jnp.int32, (total, total), 0)
    place_at = lax.broadcasted_iota(jnp.int32, (total, total), 1)
    to_core = (line >> 7) + core & 1
    to_x = (line >> 5) + x & 3
    part = line >> 4 & 1
    to_y = (line >> 2) + y & 3
    to_z = line + z & 3
    owner_row = (to_x * 2 + (to_y >> 1)) * 2 + to_core
    owner_col = to_z * 2 + (to_y & 1)
    slot_of_line = (owner_row * 8 + owner_col) * 2 + part
    line_is_slot = jnp.where(slot_of_line == place_at, 1.0, 0.0).astype(BF16)
    client_at_slot = jnp.broadcast_to(slots[...], (total, total))
    client_is_slot = jnp.where(client_at_slot == line, 1.0, 0.0).astype(BF16)
    chooser = lax.dot_general(
        line_is_slot, client_is_slot, (((1,), (1,)), ((), ())), preferred_element_type=F32
    ).astype(BF16)

    own_query.wait()
    for copy in query_copies:
        copy.wait_recv()
    entries = gathered[...].reshape(total, query_hbm.shape[1])
    chosen = jnp.dot(chooser, entries, preferred_element_type=F32).astype(BF16)
    half = total // 2

    sent = list(query_copies)
    core_copies, far_copies, near_copies, owner_copies = {}, {}, {}, {}

    def multiply(k):
        db_copies[2 * k].wait()
        db_copies[2 * k + 1].wait()
        block = db[k]
        core_out[k] = jnp.dot(chosen[half:], block, preferred_element_type=F32).astype(BF16)
        copy = remote(core_out.at[k], core_in.at[k], core_sems, (k,), partner)
        copy.start()
        core_copies[k] = copy
        own[k] = jnp.dot(chosen[:half], block, preferred_element_type=F32)

    def start_near(k, side, lines):
        target = (right, left)[side]
        copy = remote(
            near_out.at[k, side, lines],
            near_in.at[k, side, lines],
            near_sems,
            (k, side, lines),
            target,
        )
        copy.start()
        near_copies[k, side, lines] = copy

    def halve(k):
        core_copies[k].wait_recv()
        for side in range(2):
            lines = pl.ds(64 + 16 * side, 16)
            far_out[k, side] = (own[k, lines] + core_in[k, lines].astype(F32)).astype(BF16)
            copy = remote(
                far_out.at[k, side], far_in.at[k, side], far_sems, (k, side), (right, left)[side]
            )
            copy.start()
            far_copies[k, side] = copy
        for side in range(2):
            lines = pl.ds((48, 96)[side], 16)
            near_out[k, side, 1 - side] = (
                own[k, lines] + core_in[k, lines].astype(F32)
            ).astype(BF16)
            start_near(k, side, 1 - side)
        for lines in (pl.ds(32, 16), pl.ds(112, 16), pl.ds(0, 32)):
            own[k, lines] = own[k, lines] + core_in[k, lines].astype(F32)

    def pass_on(k):
        for side in range(2):
            far_copies[k, side].wait_recv()
            lines = pl.ds((32, 112)[side], 16)
            near_out[k, side, side] = (own[k, lines] + far_in[k, side].astype(F32)).astype(BF16)
            start_near(k, side, side)

    def to_owners(k):
        for part in range(2):
            for side in range(2):
                near_copies[k, side, part].wait_recv()
            lines = pl.ds(16 * part, 16)
            summed = (
                own[k, lines] + near_in[k, 0, part].astype(F32) + near_in[k, 1, part].astype(F32)
            )
            for t in range(2):
                for g in range(lane_groups):
                    lane = t * depth + g * 128
                    at = t * 2 * lane_groups + part * lane_groups + g
                    spread[pl.ds(at, 16, stride=16), :] = summed[:, lane : lane + 128]
        send_out[k] = spread[...].astype(BF16).reshape(send_out.shape[1:])
        landing = arrived.at[k, y_hi, col]
        pltpu.make_async_copy(send_out.at[k, 0], landing, owner_sems.at[1, k]).start()
        for b in range(1, 16):
            remote(send_out.at[k, b], landing, owner_sems, (k,), owners[b]).start()

    totals = [None, None]

    def pack(k):
        pltpu.make_async_copy(arrived.at[k], arrived.at[k], owner_sems.at[1, k]).wait()
        key_copies[k].wait()
        both = arrived[k, 0].astype(F32) + arrived[k, 1].astype(F32)
        switched[...] = (both * factor).reshape(switched.shape)
        for part in range(2):
            pieces = [
                switched[pl.ds(part * lane_groups + g, 16, stride=4 * lane_groups // 2), :]
                for g in range(lane_groups)
            ]
            tiles = jnp.concatenate(pieces, axis=1).astype(BF16)
            product = jnp.dot(tiles, keys[k, part], preferred_element_type=F32)
            totals[part] = product if totals[part] is None else totals[part] + product

    multiply(0)
    multiply(1)
    halve(0)
    multiply(2)
    halve(1)
    multiply(3)
    halve(2)
    pass_on(0)
    halve(3)
    pass_on(1)
    pass_on(2)
    to_owners(0)
    pass_on(3)
    to_owners(1)
    to_owners(2)
    pack(0)
    to_owners(3)
    pack(1)
    pack(2)
    pack(3)
    for part in range(2):
        out_ref[part] = totals[part]

    for copies in (core_copies, far_copies, near_copies):
        sent.extend(copies.values())
    for copy in sent:
        copy.wait_send()
    for k in range(CHUNKS):
        block = send_out.at[k, pl.ds(1, 15)]
        pltpu.make_async_copy(block, block, owner_sems.at[0, k]).wait()


def shards(database, query, slot_map, keys):
    rows_axis = lax.axis_size("row")
    factor = float(database.shape[0] * rows_axis) ** (-0.5)
    total = slot_map.shape[0]
    rows, columns = database.shape
    tile, packs = keys.shape[1:]
    width = columns // CHUNKS
    half = total // 2
    dma = pltpu.SemaphoreType.DMA
    return pl.pallas_call(
        functools.partial(kernel, factor),
        out_shape=jax.ShapeDtypeStruct((2, 16, packs), F32),
        in_specs=[pl.BlockSpec(memory_space=pltpu.HBM)] * 4,
        out_specs=pl.BlockSpec(memory_space=pltpu.VMEM),
        scratch_shapes=[
            pltpu.VMEM((1, total), jnp.int32),
            pltpu.VMEM((8, total // 8, rows), BF16),
            pltpu.VMEM((CHUNKS, rows, width), BF16),
            pltpu.VMEM((CHUNKS, 2, tile // CHUNKS, packs), BF16),
            pltpu.VMEM((CHUNKS, half, width), BF16),
            pltpu.VMEM((CHUNKS, half, width), BF16),
            pltpu.VMEM((CHUNKS, half, width), F32),
            pltpu.VMEM((CHUNKS, 2, 16, width), BF16),
            pltpu.VMEM((CHUNKS, 2, 16, width), BF16),
            pltpu.VMEM((CHUNKS, 2, 2, 16, width), BF16),
            pltpu.VMEM((CHUNKS, 2, 2, 16, width), BF16),
            pltpu.VMEM((256, 128), F32),
            pltpu.VMEM((CHUNKS, 16, 16, 128), BF16),
            pltpu.VMEM((CHUNKS, 2, 8, 16, 128), BF16),
            pltpu.VMEM((128, 128), F32),
            dma((2,)),
            dma((CHUNKS, 2)),
            dma((CHUNKS,)),
            dma((2, 7)),
            dma((2, CHUNKS)),
            dma((2, CHUNKS, 2)),
            dma((2, CHUNKS, 2, 2)),
            dma((2, CHUNKS)),
        ],
        compiler_params=pltpu.CompilerParams(
            collective_id=1, has_side_effects=True, vmem_limit_bytes=40 * 1024 * 1024
        ),
        name="answer_and_pack",
    )(slot_map.reshape(1, total), query, database, keys)


def solution(mesh):
    return jax.shard_map(
        shards,
        mesh=mesh,
        in_specs=(P("row", "col"), P("col", "row"), P(), P(("row", "col"), None, None)),
        out_specs=P(("row", "col"), None, None),
        check_vma=False,
    )
```

time: 81.3 us -> 40.6 us (0.50)
  the two profiles are of different devices: /device:TPU:0 before, /device:TPU:1 now
where the time goes in v1:
time: 40.6 us; the launch traced here: 40.3 us
  Pallas kernels  33.9 us (83%)
  local copies, waits for them, and re-layouts  6.44 us (16%)
    pallas_call x1, Pallas kernels, shards(): pl.pallas_call(functools.partial(kernel, factor), out_shape=jax.ShapeDtyp...  33.9 us
    unnamed x9, local copies, waits for them, and re-layouts  6.44 us

profile of v1, /device:TPU:1, one launch (start us, length us, event | category | flops | bytes accessed | tf_op | source)
XLA Modules:
  0.0 40.3 jit_solution(13723131463642959768)
XLA Ops:
  0.0 0.0 copy-start
  0.0 2.2 %copy-done = bf16[512,4096]{1,0:T(8,128)(2,1)S(1)} copy-done((bf16[512,4096]{1,0:T(8,128)(2,1)S(1)}, bf16[512,4096]{1,0:T(8,128)(2,1)}, u32[]{:S(2)}) %copy-start) | copy-done | bytes 4194328
  2.2 0.0 copy-start.1
  2.2 2.2 %copy-done.1 = bf16[2,2048,512]{2,1,0:T(8,128)(2,1)S(1)} copy-done((bf16[2,2048,512]{2,1,0:T(8,128)(2,1)S(1)}, bf16[2,2048,512]{2,1,0:T(8,128)(2,1)}, u32[]{:S(2)}) %copy-start.1) | copy-done | bytes 4194328
  4.4 0.0 copy-start.2
  4.4 0.8 %copy-done.2 = bf16[32,512]{1,0:T(8,128)(2,1)S(1)} copy-done((bf16[32,512]{1,0:T(8,128)(2,1)S(1)}, bf16[32,512]{1,0:T(8,128)(2,1)}, u32[]{:S(2)}) %copy-start.2) | copy-done | bytes 32792
  5.1 0.0 copy-start.3
  5.1 0.7 %copy-done.3 = s32[256]{0:T(256)S(1)} copy-done((s32[256]{0:T(256)S(1)}, s32[256]{0:T(256)}, u32[]{:S(2)}) %copy-start.3) | copy-done | bytes 1048
  5.8 33.9 %answer_and_pack.1 = f32[2,16,512]{2,1,0:T(8,128)S(1)} custom-call(s32[1,256]{1,0:T(1,128)S(1)} %bitcast.1, bf16[32,512]{1,0:T(8,128)(2,1)S(1)} %copy-done.2, bf16[512,4096]{1,0:T(8,128)(2,1)S(1)} %copy-done, bf16[2,2048,512]{2,1,0:T(8,128)(2,1)S(1)} %copy-done.1), custom_call_target="tpu_custom_call" | custom-call | tf_op jit(solution)/shard_map/answer_and_pack/pallas_call | solution.py:273
  39.7 0.6 %copy.6 = f32[2,16,512]{2,1,0:T(8,128)} copy(f32[2,16,512]{2,1,0:T(8,128)S(1)} %answer_and_pack.1) | data formatting | bytes 131072
Async XLA Ops:
  0.0 2.2 %copy-start = (bf16[512,4096]{1,0:T(8,128)(2,1)S(1)}, bf16[512,4096]{1,0:T(8,128)(2,1)}, u32[]{:S(2)}) copy-start(bf16[512,4096]{1,0:T(8,128)(2,1)} %db_hbm.1) | copy-start | bytes 12582916
  2.2 2.2 %copy-start.1 = (bf16[2,2048,512]{2,1,0:T(8,128)(2,1)S(1)}, bf16[2,2048,512]{2,1,0:T(8,128)(2,1)}, u32[]{:S(2)}) copy-start(bf16[2,2048,512]{2,1,0:T(8,128)(2,1)} %keys_hbm.1) | copy-start | bytes 12582916
  4.4 0.8 %copy-start.2 = (bf16[32,512]{1,0:T(8,128)(2,1)S(1)}, bf16[32,512]{1,0:T(8,128)(2,1)}, u32[]{:S(2)}) copy-start(bf16[32,512]{1,0:T(8,128)(2,1)} %query_hbm.1) | copy-start | bytes 98308
  5.1 0.7 %copy-start.3 = (s32[256]{0:T(256)S(1)}, s32[256]{0:T(256)}, u32[]{:S(2)}) copy-start(s32[256]{0:T(256)} %param.6) | copy-start | bytes 3076

commit v2 on v1

--- a/solution.py
+++ b/solution.py
@@ -304,7 +304,7 @@
             collective_id=1, has_side_effects=True, vmem_limit_bytes=40 * 1024 * 1024
         ),
         name="answer_and_pack",
-    )(slot_map.reshape(1, total), query, database, keys)
+    )(*(pltpu.with_memory_space_constraint(a, pltpu.HBM) for a in (slot_map.reshape(1, total), query, database, keys)))
 
 
 def solution(mesh):

time: 40.6 us -> 34 us (0.84)
  local copies, waits for them, and re-layouts: 6.44 us -> 0.63 us
  Pallas kernels: 33.9 us -> 33.2 us
    unnamed x9 -> x1, local copies, waits for them, and re-layouts: 6.44 us -> 0.63 us
    pallas_call x1, Pallas kernels: 33.9 us -> 33.2 us  [shards(): pl.pallas_call(functools.partial(kernel, factor), out_shape=jax.ShapeDtyp...]
where the time goes in v2:
time: 34 us; the launch traced here: 33.9 us
  Pallas kernels  33.2 us (98%)
  local copies, waits for them, and re-layouts  0.63 us (2%)
    pallas_call x1, Pallas kernels, shards(): pl.pallas_call(functools.partial(kernel, factor), out_shape=jax.ShapeDtyp...  33.2 us

profile of v2, /device:TPU:1, one launch (start us, length us, event | category | flops | bytes accessed | tf_op | source)
XLA Modules:
  0.0 33.9 jit_solution(9534992668183157779)
XLA Ops:
  0.0 33.2 %answer_and_pack.1 = f32[2,16,512]{2,1,0:T(8,128)S(1)} custom-call(s32[1,256]{1,0:T(1,128)} %bitcast.1, bf16[32,512]{1,0:T(8,128)(2,1)} %query_hbm.1, bf16[512,4096]{1,0:T(8,128)(2,1)} %db_hbm.1, bf16[2,2048,512]{2,1,0:T(8,128)(2,1)} %keys_hbm.1), custom_call_target="tpu_custom_call" | custom-call | tf_op jit(solution)/shard_map/answer_and_pack/pallas_call | solution.py:273
  33.2 0.6 %copy.6 = f32[2,16,512]{2,1,0:T(8,128)} copy(f32[2,16,512]{2,1,0:T(8,128)S(1)} %answer_and_pack.1) | data formatting | bytes 131072

commit v3 on v2

--- a/solution.py
+++ b/solution.py
@@ -55,6 +55,7 @@
     far_sems,
     near_sems,
     owner_sems,
+    across_sem,
 ):
     x, y, z, core = place()
     y_hi, y_lo = y // 2, lax.rem(y, 2)
@@ -71,6 +72,27 @@
             device_id=target,
             device_id_type=MESH,
         )
+
+    partner = device(x, y, z, 1 - core)
+    right, left = device(x + 1, y, z, core), device(x + 3, y, z, core)
+    owners = [device(x, y + b // 4, z + b % 4, core) for b in range(16)]
+    column_peers = []
+    for dz, other in ((2, 1), (2, 0), (1, 1), (3, 1), (1, 0), (3, 0), (0, 1)):
+        peer_y = 2 * y_hi + (1 - y_lo if other else y_lo)
+        column_peers.append(device(x, peer_y, z + dz, core))
+    across = device(x, y + 3 + 2 * y_lo, z, core)
+
+    barrier = pltpu.get_barrier_semaphore()
+    greeted = [*column_peers, across, partner, right, left]
+    for target in greeted:
+        pl.semaphore_signal(barrier, inc=1, device_id=target, device_id_type=MESH)
+    pl.semaphore_wait(barrier, len(greeted))
+
+    query_copies = []
+    for i, target in enumerate(column_peers):
+        copy = remote(query_hbm, gathered.at[col], query_sems, (i,), target)
+        copy.start()
+        query_copies.append(copy)
 
     slot_copy = pltpu.make_async_copy(slot_hbm, slots, local_sem.at[0])
     slot_copy.start()
@@ -95,28 +117,6 @@
         copy.start()
         key_copies.append(copy)
 
-    partner = device(x, y, z, 1 - core)
-    right, left = device(x + 1, y, z, core), device(x + 3, y, z, core)
-    owners = [device(x, y + b // 4, z + b % 4, core) for b in range(16)]
-    column_peers = []
-    for other in range(2):
-        peer_y = 2 * y_hi + (y_lo if other == 0 else 1 - y_lo)
-        for dz in (2, 1, 3, 0):
-            if other or dz:
-                column_peers.append(device(x, peer_y, z + dz, core))
-
-    barrier = pltpu.get_barrier_semaphore()
-    greeted = [partner, right, left, *owners[1:]]
-    for target in greeted:
-        pl.semaphore_signal(barrier, inc=1, device_id=target, device_id_type=MESH)
-    pl.semaphore_wait(barrier, len(greeted))
-
-    query_copies = []
-    for i, target in enumerate(column_peers):
-        copy = remote(query_hbm, gathered.at[col], query_sems, (i,), target)
-        copy.start()
-        query_copies.append(copy)
-
     slot_copy.wait()
     total = slots.shape[1]
     line = lax.broadcasted_iota(jnp.int32, (total, total), 0)
@@ -139,6 +139,7 @@
     own_query.wait()
     for copy in query_copies:
         copy.wait_recv()
+    pl.semaphore_signal(across_sem, inc=1, device_id=across, device_id_type=MESH)
     entries = gathered[...].reshape(total, query_hbm.shape[1])
     chosen = jnp.dot(chooser, entries, preferred_element_type=F32).astype(BF16)
     half = total // 2
@@ -206,7 +207,7 @@
                 for g in range(lane_groups):
                     lane = t * depth + g * 128
                     at = t * 2 * lane_groups + part * lane_groups + g
-                    spread[pl.ds(at, 16, stride=16), :] = summed[:, lane : lane + 128]
+                    spread[pl.ds(at, 16, stride=4 * lane_groups), :] = summed[:, lane : lane + 128]
         send_out[k] = spread[...].astype(BF16).reshape(send_out.shape[1:])
         landing = arrived.at[k, y_hi, col]
         pltpu.make_async_copy(send_out.at[k, 0], landing, owner_sems.at[1, k]).start()
@@ -222,7 +223,7 @@
         switched[...] = (both * factor).reshape(switched.shape)
         for part in range(2):
             pieces = [
-                switched[pl.ds(part * lane_groups + g, 16, stride=4 * lane_groups // 2), :]
+                switched[pl.ds(part * lane_groups + g, 16, stride=2 * lane_groups), :]
                 for g in range(lane_groups)
             ]
             tiles = jnp.concatenate(pieces, axis=1).astype(BF16)
@@ -240,6 +241,7 @@
     halve(3)
     pass_on(1)
     pass_on(2)
+    pl.semaphore_wait(across_sem, 1)
     to_owners(0)
     pass_on(3)
     to_owners(1)
@@ -287,10 +289,10 @@
             pltpu.VMEM((CHUNKS, 2, 16, width), BF16),
             pltpu.VMEM((CHUNKS, 2, 2, 16, width), BF16),
             pltpu.VMEM((CHUNKS, 2, 2, 16, width), BF16),
-            pltpu.VMEM((256, 128), F32),
-            pltpu.VMEM((CHUNKS, 16, 16, 128), BF16),
-            pltpu.VMEM((CHUNKS, 2, 8, 16, 128), BF16),
-            pltpu.VMEM((128, 128), F32),
+            pltpu.VMEM((tile // CHUNKS // 128 * 64, 128), F32),
+            pltpu.VMEM((CHUNKS, 16, tile // CHUNKS // 32, 128), BF16),
+            pltpu.VMEM((CHUNKS, 2, 8, tile // CHUNKS // 32, 128), BF16),
+            pltpu.VMEM((tile // CHUNKS // 128 * 32, 128), F32),
             dma((2,)),
             dma((CHUNKS, 2)),
             dma((CHUNKS,)),
@@ -299,6 +301,7 @@
             dma((2, CHUNKS, 2)),
             dma((2, CHUNKS, 2, 2)),
             dma((2, CHUNKS)),
+            pltpu.SemaphoreType.REGULAR,
         ],
         compiler_params=pltpu.CompilerParams(
             collective_id=1, has_side_effects=True, vmem_limit_bytes=40 * 1024 * 1024

time: 34 us -> 32.6 us (0.959)
  Pallas kernels: 33.2 us -> 31.9 us
    pallas_call x1, Pallas kernels: 33.2 us -> 31.9 us  [shards(): pl.pallas_call(functools.partial(kernel, factor), out_shape=jax.ShapeDtyp...]
where the time goes in v3:
time: 32.6 us; the launch traced here: 32.5 us
  Pallas kernels  31.9 us (98%)
  local copies, waits for them, and re-layouts  0.63 us (2%)
    pallas_call x1, Pallas kernels, shards(): pl.pallas_call(functools.partial(kernel, factor), out_shape=jax.ShapeDtyp...  31.9 us

profile of v3, /device:TPU:1, one launch (start us, length us, event | category | flops | bytes accessed | tf_op | source)
XLA Modules:
  0.0 32.5 jit_solution(8753533531531489976)
XLA Ops:
  0.0 31.9 %answer_and_pack.1 = f32[2,16,512]{2,1,0:T(8,128)S(1)} custom-call(s32[1,256]{1,0:T(1,128)} %bitcast.1, bf16[32,512]{1,0:T(8,128)(2,1)} %query_hbm.1, bf16[512,4096]{1,0:T(8,128)(2,1)} %db_hbm.1, bf16[2,2048,512]{2,1,0:T(8,128)(2,1)} %keys_hbm.1), custom_call_target="tpu_custom_call" | custom-call | tf_op jit(solution)/shard_map/answer_and_pack/pallas_call | solution.py:275
  31.9 0.6 %copy.6 = f32[2,16,512]{2,1,0:T(8,128)} copy(f32[2,16,512]{2,1,0:T(8,128)S(1)} %answer_and_pack.1) | data formatting | bytes 131072

commit v4 on v3

--- a/solution.py
+++ b/solution.py
@@ -36,8 +36,8 @@
     gathered,
     db,
     keys,
-    core_out,
-    core_in,
+    my_lines,
+    their_lines,
     own,
     far_out,
     far_in,
@@ -49,6 +49,7 @@
     switched,
     local_sem,
     db_sem,
+    db_sems,
     keys_sem,
     query_sems,
     core_sems,
@@ -98,24 +99,12 @@
     slot_copy.start()
     own_query = pltpu.make_async_copy(query_hbm, gathered.at[col], local_sem.at[1])
     own_query.start()
-    db_copies = []
-    for k in range(CHUNKS):
-        for t in range(2):
-            start = t * keys_hbm.shape[1] + k * depth
-            copy = pltpu.make_async_copy(
-                db_hbm.at[:, pl.ds(start, depth)],
-                db.at[k, :, pl.ds(t * depth, depth)],
-                db_sem.at[k, t],
-            )
-            copy.start()
-            db_copies.append(copy)
-    key_copies = []
-    for k in range(CHUNKS):
-        copy = pltpu.make_async_copy(
-            keys_hbm.at[:, pl.ds(k * depth, depth), :], keys.at[k], keys_sem.at[k]
-        )
-        copy.start()
-        key_copies.append(copy)
+    db_swap = remote(db_hbm, db.at[1], db_sems, (), partner)
+    db_swap.start()
+    db_copy = pltpu.make_async_copy(db_hbm, db.at[0], db_sem)
+    db_copy.start()
+    keys_copy = pltpu.make_async_copy(keys_hbm, keys, keys_sem)
+    keys_copy.start()
 
     slot_copy.wait()
     total = slots.shape[1]
@@ -145,17 +134,25 @@
     half = total // 2
 
     sent = list(query_copies)
-    core_copies, far_copies, near_copies, owner_copies = {}, {}, {}, {}
+    far_copies, near_copies = {}, {}
+    my_lines[...] = chosen[half:]
+    lines_copy = remote(my_lines, their_lines, core_sems, (), partner)
+    lines_copy.start()
+    sent.append(lines_copy)
+    db_copy.wait()
+    db_swap.wait_recv()
+    lines_copy.wait_recv()
+    both_lines = jnp.concatenate([chosen[:half], their_lines[...]], axis=1)
 
     def multiply(k):
-        db_copies[2 * k].wait()
-        db_copies[2 * k + 1].wait()
-        block = db[k]
-        core_out[k] = jnp.dot(chosen[half:], block, preferred_element_type=F32).astype(BF16)
-        copy = remote(core_out.at[k], core_in.at[k], core_sems, (k,), partner)
-        copy.start()
-        core_copies[k] = copy
-        own[k] = jnp.dot(chosen[:half], block, preferred_element_type=F32)
+        for t in range(2):
+            start = t * keys_hbm.shape[1] + k * depth
+            block = db[:, :, start : start + depth]
+            own[k, :, t * depth : (t + 1) * depth] = jnp.dot(
+                both_lines,
+                block.reshape(db.shape[0] * db.shape[1], depth),
+                preferred_element_type=F32,
+            )
 
     def start_near(k, side, lines):
         target = (right, left)[side]
@@ -169,24 +166,19 @@
         copy.start()
         near_copies[k, side, lines] = copy
 
-    def halve(k):
-        core_copies[k].wait_recv()
+    def send_far(k):
         for side in range(2):
-            lines = pl.ds(64 + 16 * side, 16)
-            far_out[k, side] = (own[k, lines] + core_in[k, lines].astype(F32)).astype(BF16)
+            far_out[k, side] = own[k, pl.ds(64 + 16 * side, 16)].astype(BF16)
             copy = remote(
                 far_out.at[k, side], far_in.at[k, side], far_sems, (k, side), (right, left)[side]
             )
             copy.start()
             far_copies[k, side] = copy
+
+    def send_near(k):
         for side in range(2):
-            lines = pl.ds((48, 96)[side], 16)
-            near_out[k, side, 1 - side] = (
-                own[k, lines] + core_in[k, lines].astype(F32)
-            ).astype(BF16)
+            near_out[k, side, 1 - side] = own[k, pl.ds((48, 96)[side], 16)].astype(BF16)
             start_near(k, side, 1 - side)
-        for lines in (pl.ds(32, 16), pl.ds(112, 16), pl.ds(0, 32)):
-            own[k, lines] = own[k, lines] + core_in[k, lines].astype(F32)
 
     def pass_on(k):
         for side in range(2):
@@ -194,6 +186,8 @@
             lines = pl.ds((32, 112)[side], 16)
             near_out[k, side, side] = (own[k, lines] + far_in[k, side].astype(F32)).astype(BF16)
             start_near(k, side, side)
+
+    far_first = sorted(range(16), key=lambda b: -min(b // 4, 4 - b // 4) - min(b % 4, 4 - b % 4))
 
     def to_owners(k):
         for part in range(2):
@@ -210,15 +204,20 @@
                     spread[pl.ds(at, 16, stride=4 * lane_groups), :] = summed[:, lane : lane + 128]
         send_out[k] = spread[...].astype(BF16).reshape(send_out.shape[1:])
         landing = arrived.at[k, y_hi, col]
+        for b in far_first[:-1]:
+            remote(send_out.at[k, b], landing, owner_sems, (k,), owners[b]).start()
         pltpu.make_async_copy(send_out.at[k, 0], landing, owner_sems.at[1, k]).start()
-        for b in range(1, 16):
-            remote(send_out.at[k, b], landing, owner_sems, (k,), owners[b]).start()
 
     totals = [None, None]
+
+    def finish_sends(chunks):
+        for k in chunks:
+            block = send_out.at[k, pl.ds(1, 15)]
+            pltpu.make_async_copy(block, block, owner_sems.at[0, k]).wait()
+
 
     def pack(k):
         pltpu.make_async_copy(arrived.at[k], arrived.at[k], owner_sems.at[1, k]).wait()
-        key_copies[k].wait()
         both = arrived[k, 0].astype(F32) + arrived[k, 1].astype(F32)
         switched[...] = (both * factor).reshape(switched.shape)
         for part in range(2):
@@ -227,40 +226,43 @@
                 for g in range(lane_groups)
             ]
             tiles = jnp.concatenate(pieces, axis=1).astype(BF16)
-            product = jnp.dot(tiles, keys[k, part], preferred_element_type=F32)
+            product = jnp.dot(tiles, keys[part, pl.ds(k * depth, depth)], preferred_element_type=F32)
             totals[part] = product if totals[part] is None else totals[part] + product
 
     multiply(0)
+    send_far(0)
     multiply(1)
-    halve(0)
+    send_far(1)
     multiply(2)
-    halve(1)
+    send_far(2)
     multiply(3)
-    halve(2)
+    send_far(3)
+    send_near(0)
     pass_on(0)
-    halve(3)
+    send_near(1)
     pass_on(1)
+    send_near(2)
     pass_on(2)
     pl.semaphore_wait(across_sem, 1)
     to_owners(0)
+    send_near(3)
     pass_on(3)
     to_owners(1)
     to_owners(2)
+    to_owners(3)
+    keys_copy.wait()
+    sent.append(db_swap)
+    for copies in (far_copies, near_copies):
+        sent.extend(copies.values())
+    for copy in sent:
+        copy.wait_send()
     pack(0)
-    to_owners(3)
     pack(1)
     pack(2)
+    finish_sends(range(0, 4))
     pack(3)
     for part in range(2):
         out_ref[part] = totals[part]
-
-    for copies in (core_copies, far_copies, near_copies):
-        sent.extend(copies.values())
-    for copy in sent:
-        copy.wait_send()
-    for k in range(CHUNKS):
-        block = send_out.at[k, pl.ds(1, 15)]
-        pltpu.make_async_copy(block, block, owner_sems.at[0, k]).wait()
 
 
 def shards(database, query, slot_map, keys):
@@ -280,10 +282,10 @@
         scratch_shapes=[
             pltpu.VMEM((1, total), jnp.int32),
             pltpu.VMEM((8, total // 8, rows), BF16),
-            pltpu.VMEM((CHUNKS, rows, width), BF16),
-            pltpu.VMEM((CHUNKS, 2, tile // CHUNKS, packs), BF16),
-            pltpu.VMEM((CHUNKS, half, width), BF16),
-            pltpu.VMEM((CHUNKS, half, width), BF16),
+            pltpu.VMEM((2, rows, columns), BF16),
+            pltpu.VMEM((2, tile, packs), BF16),
+            pltpu.VMEM((half, rows), BF16),
+            pltpu.VMEM((half, rows), BF16),
             pltpu.VMEM((CHUNKS, half, width), F32),
             pltpu.VMEM((CHUNKS, 2, 16, width), BF16),
             pltpu.VMEM((CHUNKS, 2, 16, width), BF16),
@@ -294,10 +296,11 @@
             pltpu.VMEM((CHUNKS, 2, 8, tile // CHUNKS // 32, 128), BF16),
             pltpu.VMEM((tile // CHUNKS // 128 * 32, 128), F32),
             dma((2,)),
-            dma((CHUNKS, 2)),
-            dma((CHUNKS,)),
+            dma(()),
+            dma((2,)),
+            dma(()),
             dma((2, 7)),
-            dma((2, CHUNKS)),
+            dma((2,)),
             dma((2, CHUNKS, 2)),
             dma((2, CHUNKS, 2, 2)),
             dma((2, CHUNKS)),

time: 32.6 us -> 31.9 us (0.979)
  Pallas kernels: 31.9 us -> 30.9 us
    pallas_call x1, Pallas kernels: 31.9 us -> 30.9 us  [shards(): pl.pallas_call(functools.partial(kernel, factor), out_shape=jax.ShapeDtyp...]
where the time goes in v4:
time: 31.9 us; the launch traced here: 31.5 us
  Pallas kernels  30.9 us (97%)
  local copies, waits for them, and re-layouts  0.63 us (2%)
    pallas_call x1, Pallas kernels, shards(): pl.pallas_call(functools.partial(kernel, factor), out_shape=jax.ShapeDtyp...  30.9 us

profile of v4, /device:TPU:1, one launch (start us, length us, event | category | flops | bytes accessed | tf_op | source)
XLA Modules:
  0.0 31.5 jit_solution(11587461091527668279)
XLA Ops:
  0.0 30.9 %answer_and_pack.1 = f32[2,16,512]{2,1,0:T(8,128)S(1)} custom-call(s32[1,256]{1,0:T(1,128)} %bitcast.1, bf16[32,512]{1,0:T(8,128)(2,1)} %query_hbm.1, bf16[512,4096]{1,0:T(8,128)(2,1)} %db_hbm.1, bf16[2,2048,512]{2,1,0:T(8,128)(2,1)} %keys_hbm.1), custom_call_target="tpu_custom_call" | custom-call | tf_op jit(solution)/shard_map/answer_and_pack/pallas_call | solution.py:277
  30.9 0.6 %copy.6 = f32[2,16,512]{2,1,0:T(8,128)} copy(f32[2,16,512]{2,1,0:T(8,128)S(1)} %answer_and_pack.1) | data formatting | bytes 131072

commit v5 on v4

--- a/solution.py
+++ b/solution.py
@@ -56,7 +56,11 @@
     far_sems,
     near_sems,
     owner_sems,
+    direct_out,
+    direct_in,
+    direct_sems,
     across_sem,
+    plane_sem,
 ):
     x, y, z, core = place()
     y_hi, y_lo = y // 2, lax.rem(y, 2)
@@ -208,6 +212,36 @@
             remote(send_out.at[k, b], landing, owner_sems, (k,), owners[b]).start()
         pltpu.make_async_copy(send_out.at[k, 0], landing, owner_sems.at[1, k]).start()
 
+    def direct(origins):
+        for origin in origins:
+            if origin:
+                side = origin - 1
+                copy = far_copies[CHUNKS - 1, side]
+                copy.wait_recv()
+            for part in range(2):
+                first = (0, 32, 96)[origin] + 16 * part
+                summed = own[CHUNKS - 1, pl.ds(first, 16)]
+                if origin and part == side:
+                    summed = summed + far_in[CHUNKS - 1, side].astype(F32)
+                for t in range(2):
+                    for g in range(lane_groups):
+                        lane = t * depth + g * 128
+                        at = t * 2 * lane_groups + part * lane_groups + g
+                        spread[pl.ds(at, 16, stride=4 * lane_groups), :] = summed[
+                            :, lane : lane + 128
+                        ]
+            direct_out[origin] = spread[...].astype(BF16).reshape(direct_out.shape[1:])
+        for b in far_first:
+            for origin in origins:
+                landing = direct_in.at[origin, y_hi, col]
+                if b or origin:
+                    target = device(x + (0, 1, 3)[origin], y + b // 4, z + b % 4, core)
+                    remote(direct_out.at[origin, b], landing, direct_sems, (origin,), target).start()
+                else:
+                    pltpu.make_async_copy(
+                        direct_out.at[0, 0], landing, direct_sems.at[1, 0]
+                    ).start()
+
     totals = [None, None]
 
     def finish_sends(chunks):
@@ -217,8 +251,16 @@
 
 
     def pack(k):
-        pltpu.make_async_copy(arrived.at[k], arrived.at[k], owner_sems.at[1, k]).wait()
-        both = arrived[k, 0].astype(F32) + arrived[k, 1].astype(F32)
+        if k < CHUNKS - 1:
+            pltpu.make_async_copy(arrived.at[k], arrived.at[k], owner_sems.at[1, k]).wait()
+            both = arrived[k, 0].astype(F32) + arrived[k, 1].astype(F32)
+        else:
+            both = None
+            for origin in (0, 1, 2):
+                block = direct_in.at[origin]
+                pltpu.make_async_copy(block, block, direct_sems.at[1, origin]).wait()
+                pair = direct_in[origin, 0].astype(F32) + direct_in[origin, 1].astype(F32)
+                both = pair if both is None else both + pair
         switched[...] = (both * factor).reshape(switched.shape)
         for part in range(2):
             pieces = [
@@ -229,27 +271,29 @@
             product = jnp.dot(tiles, keys[part, pl.ds(k * depth, depth)], preferred_element_type=F32)
             totals[part] = product if totals[part] is None else totals[part] + product
 
+    multiply(3)
+    send_far(3)
     multiply(0)
     send_far(0)
     multiply(1)
     send_far(1)
     multiply(2)
     send_far(2)
-    multiply(3)
-    send_far(3)
     send_near(0)
+    send_near(1)
     pass_on(0)
-    send_near(1)
+    pl.semaphore_wait(across_sem, 1)
+    for target in (right, left):
+        pl.semaphore_signal(plane_sem, inc=1, device_id=target, device_id_type=MESH)
+    send_near(2)
     pass_on(1)
-    send_near(2)
     pass_on(2)
-    pl.semaphore_wait(across_sem, 1)
+    pl.semaphore_wait(plane_sem, 2)
+    direct((0,))
+    direct((1, 2))
     to_owners(0)
-    send_near(3)
-    pass_on(3)
     to_owners(1)
     to_owners(2)
-    to_owners(3)
     keys_copy.wait()
     sent.append(db_swap)
     for copies in (far_copies, near_copies):
@@ -259,7 +303,10 @@
     pack(0)
     pack(1)
     pack(2)
-    finish_sends(range(0, 4))
+    finish_sends(range(CHUNKS - 1))
+    for origin in range(3):
+        block = direct_out.at[origin] if origin else direct_out.at[0, pl.ds(1, 15)]
+        pltpu.make_async_copy(block, block, direct_sems.at[0, origin]).wait()
     pack(3)
     for part in range(2):
         out_ref[part] = totals[part]
@@ -289,11 +336,11 @@
             pltpu.VMEM((CHUNKS, half, width), F32),
             pltpu.VMEM((CHUNKS, 2, 16, width), BF16),
             pltpu.VMEM((CHUNKS, 2, 16, width), BF16),
-            pltpu.VMEM((CHUNKS, 2, 2, 16, width), BF16),
-            pltpu.VMEM((CHUNKS, 2, 2, 16, width), BF16),
+            pltpu.VMEM((CHUNKS - 1, 2, 2, 16, width), BF16),
+            pltpu.VMEM((CHUNKS - 1, 2, 2, 16, width), BF16),
             pltpu.VMEM((tile // CHUNKS // 128 * 64, 128), F32),
-            pltpu.VMEM((CHUNKS, 16, tile // CHUNKS // 32, 128), BF16),
-            pltpu.VMEM((CHUNKS, 2, 8, tile // CHUNKS // 32, 128), BF16),
+            pltpu.VMEM((CHUNKS - 1, 16, tile // CHUNKS // 32, 128), BF16),
+            pltpu.VMEM((CHUNKS - 1, 2, 8, tile // CHUNKS // 32, 128), BF16),
             pltpu.VMEM((tile // CHUNKS // 128 * 32, 128), F32),
             dma((2,)),
             dma(()),
@@ -302,8 +349,12 @@
             dma((2, 7)),
             dma((2,)),
             dma((2, CHUNKS, 2)),
-            dma((2, CHUNKS, 2, 2)),
-            dma((2, CHUNKS)),
+            dma((2, CHUNKS - 1, 2, 2)),
+            dma((2, CHUNKS - 1)),
+            pltpu.VMEM((3, 16, tile // CHUNKS // 32, 128), BF16),
+            pltpu.VMEM((3, 2, 8, tile // CHUNKS // 32, 128), BF16),
+            dma((2, 3)),
+            pltpu.SemaphoreType.REGULAR,
             pltpu.SemaphoreType.REGULAR,
         ],
         compiler_params=pltpu.CompilerParams(

time: 31.9 us -> 31.1 us (0.975)
  Pallas kernels: 30.9 us -> 30.3 us
    pallas_call x1, Pallas kernels: 30.9 us -> 30.3 us  [shards(): pl.pallas_call(functools.partial(kernel, factor), out_shape=jax.ShapeDtyp...]
where the time goes in v5:
time: 31.1 us; the launch traced here: 31 us
  Pallas kernels  30.3 us (97%)
  local copies, waits for them, and re-layouts  0.63 us (2%)
    pallas_call x1, Pallas kernels, shards(): pl.pallas_call(functools.partial(kernel, factor), out_shape=jax.ShapeDtyp...  30.3 us
    unnamed x1, local copies, waits for them, and re-layouts  0.63 us

profile of v5, /device:TPU:1, one launch (start us, length us, event | category | flops | bytes accessed | tf_op | source)
XLA Modules:
  0.0 31.0 jit_solution(13348011178963381306)
XLA Ops:
  0.0 30.3 %answer_and_pack.1 = f32[2,16,512]{2,1,0:T(8,128)S(1)} custom-call(s32[1,256]{1,0:T(1,128)} %bitcast.1, bf16[32,512]{1,0:T(8,128)(2,1)} %query_hbm.1, bf16[512,4096]{1,0:T(8,128)(2,1)} %db_hbm.1, bf16[2,2048,512]{2,1,0:T(8,128)(2,1)} %keys_hbm.1), custom_call_target="tpu_custom_call" | custom-call | tf_op jit(solution)/shard_map/answer_and_pack/pallas_call | solution.py:324
  30.3 0.6 %copy.6 = f32[2,16,512]{2,1,0:T(8,128)} copy(f32[2,16,512]{2,1,0:T(8,128)S(1)} %answer_and_pack.1) | data formatting | bytes 131072

commit v6 on v5

--- a/solution.py
+++ b/solution.py
@@ -9,6 +9,7 @@
 
 MESH = pl.DeviceIdType.MESH
 CHUNKS = 4
+STAGED = 3
 F32 = jnp.float32
 BF16 = jnp.bfloat16
 
@@ -214,23 +215,24 @@
 
     def direct(origins):
         for origin in origins:
-            if origin:
+            for k in range(STAGED, CHUNKS):
                 side = origin - 1
-                copy = far_copies[CHUNKS - 1, side]
-                copy.wait_recv()
-            for part in range(2):
-                first = (0, 32, 96)[origin] + 16 * part
-                summed = own[CHUNKS - 1, pl.ds(first, 16)]
-                if origin and part == side:
-                    summed = summed + far_in[CHUNKS - 1, side].astype(F32)
-                for t in range(2):
-                    for g in range(lane_groups):
-                        lane = t * depth + g * 128
-                        at = t * 2 * lane_groups + part * lane_groups + g
-                        spread[pl.ds(at, 16, stride=4 * lane_groups), :] = summed[
-                            :, lane : lane + 128
-                        ]
-            direct_out[origin] = spread[...].astype(BF16).reshape(direct_out.shape[1:])
+                if origin:
+                    far_copies[k, side].wait_recv()
+                for part in range(2):
+                    summed = own[k, pl.ds((0, 32, 96)[origin] + 16 * part, 16)]
+                    if origin and part == side:
+                        summed = summed + far_in[k, side].astype(F32)
+                    for t in range(2):
+                        for g in range(lane_groups):
+                            lane = t * depth + g * 128
+                            at = t * 2 * lane_groups + part * lane_groups + g
+                            spread[pl.ds(at, 16, stride=4 * lane_groups), :] = summed[
+                                :, lane : lane + 128
+                            ]
+                direct_out[origin, :, k - STAGED] = spread[...].astype(BF16).reshape(
+                    16, *direct_out.shape[3:]
+                )
         for b in far_first:
             for origin in origins:
                 landing = direct_in.at[origin, y_hi, col]
@@ -251,15 +253,17 @@
 
 
     def pack(k):
-        if k < CHUNKS - 1:
+        if k < STAGED:
             pltpu.make_async_copy(arrived.at[k], arrived.at[k], owner_sems.at[1, k]).wait()
             both = arrived[k, 0].astype(F32) + arrived[k, 1].astype(F32)
         else:
             both = None
             for origin in (0, 1, 2):
                 block = direct_in.at[origin]
-                pltpu.make_async_copy(block, block, direct_sems.at[1, origin]).wait()
-                pair = direct_in[origin, 0].astype(F32) + direct_in[origin, 1].astype(F32)
+                if k == STAGED:
+                    pltpu.make_async_copy(block, block, direct_sems.at[1, origin]).wait()
+                pair = direct_in[origin, 0, :, k - STAGED].astype(F32)
+                pair = pair + direct_in[origin, 1, :, k - STAGED].astype(F32)
                 both = pair if both is None else both + pair
         switched[...] = (both * factor).reshape(switched.shape)
         for part in range(2):
@@ -280,13 +284,13 @@
     multiply(2)
     send_far(2)
     send_near(0)
+    pass_on(0)
     send_near(1)
-    pass_on(0)
     pl.semaphore_wait(across_sem, 1)
     for target in (right, left):
         pl.semaphore_signal(plane_sem, inc=1, device_id=target, device_id_type=MESH)
+    pass_on(1)
     send_near(2)
-    pass_on(1)
     pass_on(2)
     pl.semaphore_wait(plane_sem, 2)
     direct((0,))
@@ -303,7 +307,7 @@
     pack(0)
     pack(1)
     pack(2)
-    finish_sends(range(CHUNKS - 1))
+    finish_sends(range(STAGED))
     for origin in range(3):
         block = direct_out.at[origin] if origin else direct_out.at[0, pl.ds(1, 15)]
         pltpu.make_async_copy(block, block, direct_sems.at[0, origin]).wait()
@@ -336,11 +340,11 @@
             pltpu.VMEM((CHUNKS, half, width), F32),
             pltpu.VMEM((CHUNKS, 2, 16, width), BF16),
             pltpu.VMEM((CHUNKS, 2, 16, width), BF16),
-            pltpu.VMEM((CHUNKS - 1, 2, 2, 16, width), BF16),
-            pltpu.VMEM((CHUNKS - 1, 2, 2, 16, width), BF16),
+            pltpu.VMEM((STAGED, 2, 2, 16, width), BF16),
+            pltpu.VMEM((STAGED, 2, 2, 16, width), BF16),
             pltpu.VMEM((tile // CHUNKS // 128 * 64, 128), F32),
-            pltpu.VMEM((CHUNKS - 1, 16, tile // CHUNKS // 32, 128), BF16),
-            pltpu.VMEM((CHUNKS - 1, 2, 8, tile // CHUNKS // 32, 128), BF16),
+            pltpu.VMEM((STAGED, 16, tile // CHUNKS // 32, 128), BF16),
+            pltpu.VMEM((STAGED, 2, 8, tile // CHUNKS // 32, 128), BF16),
             pltpu.VMEM((tile // CHUNKS // 128 * 32, 128), F32),
             dma((2,)),
             dma(()),
@@ -349,10 +353,10 @@
             dma((2, 7)),
             dma((2,)),
             dma((2, CHUNKS, 2)),
-            dma((2, CHUNKS - 1, 2, 2)),
-            dma((2, CHUNKS - 1)),
-            pltpu.VMEM((3, 16, tile // CHUNKS // 32, 128), BF16),
-            pltpu.VMEM((3, 2, 8, tile // CHUNKS // 32, 128), BF16),
+            dma((2, STAGED, 2, 2)),
+            dma((2, STAGED)),
+            pltpu.VMEM((3, 16, CHUNKS - STAGED, tile // CHUNKS // 32, 128), BF16),
+            pltpu.VMEM((3, 2, 8, CHUNKS - STAGED, tile // CHUNKS // 32, 128), BF16),
             dma((2, 3)),
             pltpu.SemaphoreType.REGULAR,
             pltpu.SemaphoreType.REGULAR,

time: 31.1 us -> 30.8 us (level)
  no operation moved by 1% of the time
where the time goes in v6:
time: 30.8 us; the launch traced here: 30.7 us
  Pallas kernels  30.1 us (98%)
  local copies, waits for them, and re-layouts  0.63 us (2%)
    pallas_call x1, Pallas kernels, shards(): pl.pallas_call(functools.partial(kernel, factor), out_shape=jax.ShapeDtyp...  30.1 us
    unnamed x1, local copies, waits for them, and re-layouts  0.63 us

profile of v6, /device:TPU:1, one launch (start us, length us, event | category | flops | bytes accessed | tf_op | source)
XLA Modules:
  0.0 30.7 jit_solution(1547938865391933943)
XLA Ops:
  0.0 30.1 %answer_and_pack.1 = f32[2,16,512]{2,1,0:T(8,128)S(1)} custom-call(s32[1,256]{1,0:T(1,128)} %bitcast.1, bf16[32,512]{1,0:T(8,128)(2,1)} %query_hbm.1, bf16[512,4096]{1,0:T(8,128)(2,1)} %db_hbm.1, bf16[2,2048,512]{2,1,0:T(8,128)(2,1)} %keys_hbm.1), custom_call_target="tpu_custom_call" | custom-call | tf_op jit(solution)/shard_map/answer_and_pack/pallas_call | solution.py:328
  30.1 0.6 %copy.6 = f32[2,16,512]{2,1,0:T(8,128)} copy(f32[2,16,512]{2,1,0:T(8,128)S(1)} %answer_and_pack.1) | data formatting | bytes 131072

commit v7 on v6

--- a/solution.py
+++ b/solution.py
@@ -133,21 +133,24 @@
     own_query.wait()
     for copy in query_copies:
         copy.wait_recv()
-    pl.semaphore_signal(across_sem, inc=1, device_id=across, device_id_type=MESH)
     entries = gathered[...].reshape(total, query_hbm.shape[1])
-    chosen = jnp.dot(chooser, entries, preferred_element_type=F32).astype(BF16)
     half = total // 2
+
+    def choose(lines):
+        return jnp.dot(lines, entries, preferred_element_type=F32).astype(BF16)
 
     sent = list(query_copies)
     far_copies, near_copies = {}, {}
-    my_lines[...] = chosen[half:]
+    my_lines[...] = choose(chooser[half:])
     lines_copy = remote(my_lines, their_lines, core_sems, (), partner)
     lines_copy.start()
+    pl.semaphore_signal(across_sem, inc=1, device_id=across, device_id_type=MESH)
+    own_lines = choose(chooser[:half])
     sent.append(lines_copy)
     db_copy.wait()
     db_swap.wait_recv()
     lines_copy.wait_recv()
-    both_lines = jnp.concatenate([chosen[:half], their_lines[...]], axis=1)
+    both_lines = jnp.concatenate([own_lines, their_lines[...]], axis=1)
 
     def multiply(k):
         for t in range(2):

time: 30.8 us -> 30.8 us (level)
  no operation moved by 1% of the time
where the time goes in v7:
time: 30.8 us; the launch traced here: 30.7 us
  Pallas kernels  30.1 us (98%)
  local copies, waits for them, and re-layouts  0.63 us (2%)
    pallas_call x1, Pallas kernels, shards(): pl.pallas_call(functools.partial(kernel, factor), out_shape=jax.ShapeDtyp...  30.1 us
    unnamed x1, local copies, waits for them, and re-layouts  0.63 us

profile of v7, /device:TPU:1, one launch (start us, length us, event | category | flops | bytes accessed | tf_op | source)
XLA Modules:
  0.0 30.7 jit_solution(4301534173967064252)
XLA Ops:
  0.0 30.1 %answer_and_pack.1 = f32[2,16,512]{2,1,0:T(8,128)S(1)} custom-call(s32[1,256]{1,0:T(1,128)} %bitcast.1, bf16[32,512]{1,0:T(8,128)(2,1)} %query_hbm.1, bf16[512,4096]{1,0:T(8,128)(2,1)} %db_hbm.1, bf16[2,2048,512]{2,1,0:T(8,128)(2,1)} %keys_hbm.1), custom_call_target="tpu_custom_call" | custom-call | tf_op jit(solution)/shard_map/answer_and_pack/pallas_call | solution.py:331
  30.1 0.6 %copy.6 = f32[2,16,512]{2,1,0:T(8,128)} copy(f32[2,16,512]{2,1,0:T(8,128)S(1)} %answer_and_pack.1) | data formatting | bytes 131072

commit v8 on v7

--- a/solution.py
+++ b/solution.py
@@ -295,8 +295,8 @@
     pass_on(1)
     send_near(2)
     pass_on(2)
+    direct((0,))
     pl.semaphore_wait(plane_sem, 2)
-    direct((0,))
     direct((1, 2))
     to_owners(0)
     to_owners(1)

time: 30.8 us -> 30.8 us (level)
  no operation moved by 1% of the time
where the time goes in v8:
time: 30.8 us; the launch traced here: 30.7 us
  Pallas kernels  30.1 us (98%)
  local copies, waits for them, and re-layouts  0.63 us (2%)
    pallas_call x1, Pallas kernels, shards(): pl.pallas_call(functools.partial(kernel, factor), out_shape=jax.ShapeDtyp...  30.1 us
    unnamed x1, local copies, waits for them, and re-layouts  0.63 us

profile of v8, /device:TPU:1, one launch (start us, length us, event | category | flops | bytes accessed | tf_op | source)
XLA Modules:
  0.0 30.7 jit_solution(559632426268157631)
XLA Ops:
  0.0 30.1 %answer_and_pack.1 = f32[2,16,512]{2,1,0:T(8,128)S(1)} custom-call(s32[1,256]{1,0:T(1,128)} %bitcast.1, bf16[32,512]{1,0:T(8,128)(2,1)} %query_hbm.1, bf16[512,4096]{1,0:T(8,128)(2,1)} %db_hbm.1, bf16[2,2048,512]{2,1,0:T(8,128)(2,1)} %keys_hbm.1), custom_call_target="tpu_custom_call" | custom-call | tf_op jit(solution)/shard_map/answer_and_pack/pallas_call | solution.py:331
  30.1 0.6 %copy.6 = f32[2,16,512]{2,1,0:T(8,128)} copy(f32[2,16,512]{2,1,0:T(8,128)S(1)} %answer_and_pack.1) | data formatting | bytes 131072
